TPU v7x, 512 devices: a whole 4x4x16 slice. The times are simulated.
512 devices in a mesh: dp: 32 (over x, y, core), expert: 16 (over z).
Axes of the slice: x: 4, y: 4, z: 16, core: 2. Of those that a mesh axis runs over, the one named last changes fastest.
Arguments:
- tokens: bfloat16 [4096, 2048], P('dp', 'expert'), may hold values from -6 to 6
- cotangent: bfloat16 [4096, 2048], P('dp', 'expert'), may hold values from -6 to 6
- expert_ids: int32 [4096, 8], P('dp'), may hold values from 0 to 127, all different within a row; in each aligned block of 128 rows (0 to 127, 128 to 255, ...) at most 16 rows name the same one
- gate_weights: float32 [4096, 8], P('dp'), may hold values from 0.05 to 1
- w_gate: bfloat16 [512, 192, 2048], P(('dp', 'expert')), may hold values from -0.125 to 0.125
- w_up: bfloat16 [512, 192, 2048], P(('dp', 'expert')), may hold values from -0.125 to 0.125
- w_down: bfloat16 [512, 192, 2048], P(('dp', 'expert')), may hold values from -0.21875 to 0.21875
Outputs:
- layer_out: bfloat16 [4096, 2048], P('dp', 'expert')
- grad_tokens: bfloat16 [4096, 2048], P('dp', 'expert')
- grad_gates: float32 [4096, 8], P('dp')
- grad_w_gate: bfloat16 [512, 192, 2048], P(('dp', 'expert'))
- grad_w_up: bfloat16 [512, 192, 2048], P(('dp', 'expert'))
- grad_w_down: bfloat16 [512, 192, 2048], P(('dp', 'expert'))
Inputs may be any that keep to these rules, and one draw needn't show every extreme that they name: `expert_ids`: each row names 8 different experts. In each aligned block of 128 rows (the rows of one index of dp) no expert is named by more than 16 rows, and in some block an expert is named by exactly 16 rows.
All inputs are finite; a program needn't handle non-finite values.
Results may differ from a plain program's by a relative error of at most 0.0064.
Values may be sent and summed in bfloat16 or wider, within the bound.
No kernel may reach another device: no remote copies, remote signals or barrier semaphores. Data moves between devices by JAX's collectives and lax.ppermute only.
A program may use at most 64 MiB of HBM per device.

v0:
```python
import jax
import jax.numpy as jnp
from jax import lax
from jax.sharding import PartitionSpec as P

SHARDS = 4


def silu_parts(preact):
    sigmoid_of = jax.nn.sigmoid(preact)
    activated = preact * sigmoid_of
    derivative = sigmoid_of * (1.0 + preact * (1.0 - sigmoid_of))
    return (activated, derivative)


def contract_last(first_op, second_op):
    return lax.dot_general(
        first_op, second_op, (((1,), (1,)), ((), ())), preferred_element_type=jnp.float32
    )


def contract_first(first_op, second_op):
    return lax.dot_general(
        first_op, second_op, (((0,), (0,)), ((), ())), preferred_element_type=jnp.float32
    )


def expert_rows(rows_x, rows_do, gate_w, up_w, down_w):
    pre_gate = contract_last(rows_x, gate_w)
    pre_up = contract_last(rows_x, up_w)
    activated, derivative = silu_parts(pre_gate)
    hidden = (activated * pre_up).astype(jnp.bfloat16)
    part_out = jnp.dot(hidden, down_w, preferred_element_type=jnp.float32).astype(jnp.bfloat16)
    d_hidden = contract_last(rows_do, down_w)
    d_pre_gate = (d_hidden * pre_up * derivative).astype(jnp.bfloat16)
    d_pre_up = (d_hidden * activated).astype(jnp.bfloat16)
    part_grad = (
        jnp.dot(d_pre_gate, gate_w, preferred_element_type=jnp.float32)
        + jnp.dot(d_pre_up, up_w, preferred_element_type=jnp.float32)
    ).astype(jnp.bfloat16)
    gradients = (
        contract_first(d_pre_gate, rows_x),
        contract_first(d_pre_up, rows_x),
        contract_first(hidden, rows_do),
    )
    return (part_out, part_grad, gradients)


def forward_part(rows_x, gate_w, up_w, down_w):
    pre_gate = contract_last(rows_x, gate_w)
    pre_up = contract_last(rows_x, up_w)
    activated, derivative = silu_parts(pre_gate)
    hidden = (activated * pre_up).astype(jnp.bfloat16)
    part_out = jnp.dot(hidden, down_w, preferred_element_type=jnp.float32).astype(jnp.bfloat16)
    return (pre_up, activated, derivative, hidden, part_out)


def backward_part(rows_x, rows_do, gate_w, up_w, down_w, pre_up, activated, derivative, hidden):
    d_hidden = contract_last(rows_do, down_w)
    d_pre_gate = (d_hidden * pre_up * derivative).astype(jnp.bfloat16)
    d_pre_up = (d_hidden * activated).astype(jnp.bfloat16)
    part_grad = (
        jnp.dot(d_pre_gate, gate_w, preferred_element_type=jnp.float32)
        + jnp.dot(d_pre_up, up_w, preferred_element_type=jnp.float32)
    ).astype(jnp.bfloat16)
    gradients = (
        contract_first(d_pre_gate, rows_x),
        contract_first(d_pre_up, rows_x),
        contract_first(hidden, rows_do),
    )
    return (part_grad, gradients)


def per_device(tokens, cotangent, expert_ids, gate_weights, w_gate, w_up, w_down):
    full_x = lax.all_gather(tokens, "expert", axis=1, tiled=True)
    full_dy = lax.all_gather(cotangent, "expert", axis=1, tiled=True)
    dp_count = lax.axis_size("dp")
    column_count = lax.axis_size("expert")
    column = lax.axis_index("expert")
    tok_count, chosen = expert_ids.shape
    features = full_x.shape[1]
    experts_all = dp_count * column_count // SHARDS
    capacity = min(tok_count, max(2, 2 * tok_count * chosen // experts_all))
    per_row = column_count // SHARDS
    assigned = tok_count * chosen
    flat_ids = expert_ids.reshape(-1)
    flat_gates = gate_weights.reshape(-1)
    slot_total = dp_count * capacity
    owned_here = flat_ids % per_row == column // SHARDS
    target_row = flat_ids // per_row
    onehot = (
        (target_row[:, None] == jnp.arange(dp_count, dtype=jnp.int32)[None, :])
        & owned_here[:, None]
    ).astype(jnp.bfloat16)
    order = jnp.arange(assigned, dtype=jnp.int32)
    earlier = (order[:, None] > order[None, :]).astype(jnp.bfloat16)
    counts = jnp.dot(earlier, onehot, preferred_element_type=jnp.float32)
    rank_of = jnp.sum(counts * onehot.astype(jnp.float32), axis=1).astype(jnp.int32)
    target = jnp.where(owned_here, target_row * capacity + rank_of, slot_total)
    picks = target[None, :] == jnp.arange(slot_total, dtype=jnp.int32)[:, None]
    slot_gate = jnp.sum(jnp.where(picks, flat_gates[None, :], 0.0), axis=1)
    token_of = jnp.any(picks.reshape(slot_total, tok_count, chosen), axis=2)
    token_pick = token_of.astype(jnp.bfloat16)
    send_x = jnp.dot(token_pick, full_x, preferred_element_type=jnp.bfloat16).reshape(
        dp_count, capacity, features
    )
    slot_dy = jnp.dot(token_pick, full_dy, preferred_element_type=jnp.float32)
    send_do = (
        (slot_gate[:, None] * slot_dy).astype(jnp.bfloat16).reshape(dp_count, capacity, features)
    )
    weights = (w_gate[0], w_up[0], w_down[0])
    recv_x = lax.all_to_all(send_x, "dp", split_axis=0, concat_axis=0, tiled=True)
    recv_do = lax.all_to_all(send_do, "dp", split_axis=0, concat_axis=0, tiled=True)
    rows_x = recv_x.reshape(slot_total, features)
    rows_do = recv_do.reshape(slot_total, features)
    pre_up, activated, derivative, hidden, part_out = forward_part(rows_x, *weights)
    part_out, hidden, rows_do = lax.optimization_barrier((part_out, hidden, rows_do))
    part_grad, gradients = backward_part(
        rows_x, rows_do, *weights, pre_up, activated, derivative, hidden
    )
    back = lax.all_to_all(
        jnp.concatenate(
            [
                part_out.reshape(dp_count, capacity, features),
                part_grad.reshape(dp_count, capacity, features),
            ],
            axis=1,
        ),
        "dp",
        split_axis=0,
        concat_axis=0,
        tiled=True,
    )
    back_out = back[:, :capacity].reshape(slot_total, features)
    back_grad = back[:, capacity:].reshape(slot_total, features)
    gated_pick = token_pick.astype(jnp.float32) * slot_gate[:, None]
    out_part = lax.dot_general(
        gated_pick,
        back_out.astype(jnp.float32),
        (((0,), (0,)), ((), ())),
        precision=lax.Precision.HIGHEST,
        preferred_element_type=jnp.float32,
    )
    grad_part = contract_first(token_pick, back_grad)
    dy_rows = jnp.dot(token_pick, full_dy, preferred_element_type=jnp.bfloat16)
    gate_terms = jnp.sum(dy_rows.astype(jnp.float32) * back_out.astype(jnp.float32), axis=1)
    gate_part = jnp.sum(jnp.where(picks, gate_terms[:, None], 0.0), axis=0).reshape(
        tok_count, chosen
    )
    summed = lax.psum_scatter(
        jnp.stack([out_part, grad_part]), "expert", scatter_dimension=2, tiled=True
    )
    gate_all = lax.all_gather(gate_part, "expert", axis=0, tiled=False)
    grad_gates = gate_all[0]
    for source in range(1, column_count):
        grad_gates = grad_gates + gate_all[source]
    return (
        summed[0].astype(jnp.bfloat16),
        summed[1].astype(jnp.bfloat16),
        grad_gates,
        gradients[0].astype(jnp.bfloat16)[None],
        gradients[1].astype(jnp.bfloat16)[None],
        gradients[2].astype(jnp.bfloat16)[None],
    )


def solution(mesh):
    placed = (
        P("dp", "expert"),
        P("dp", "expert"),
        P("dp", None),
        P("dp", None),
        P(("dp", "expert"), None, None),
        P(("dp", "expert"), None, None),
        P(("dp", "expert"), None, None),
    )
    return jax.shard_map(
        per_device,
        mesh=mesh,
        in_specs=placed,
        out_specs=(
            P("dp", "expert"),
            P("dp", "expert"),
            P("dp", None),
            P(("dp", "expert"), None, None),
            P(("dp", "expert"), None, None),
            P(("dp", "expert"), None, None),
        ),
        check_vma=False,
    )
```

profile of v0, /device:TPU:4, one launch (start us, length us, event | category | flops | bytes accessed | tf_op | source)
XLA Modules:
  0.0 265.1 jit_solution(6410177237351230202)
XLA Ops:
  7.2 0.0 copy-start
  7.2 0.9 copy.28
  8.0 0.1 reshape.163
  8.2 0.5 fusion.6
  8.7 0.1 convert_element_type.69
  8.8 0.1 fusion.30
  9.0 0.9 fusion.4
  9.9 38.8 %all_gather.9 = bf16[128,2048]{1,0:T(8,128)(2,1)S(1)} all-gather(bf16[128,128]{1,0:T(8,128)(2,1)} %param.7), channel_id=1, replica_groups=mesh['dp'=32,'expert'=16] {'expert'}, dimensions={1}, use_global_device_ids=true | all-gather | bytes 557056 | tf_op jit(solution)/shard_map/all_gather | solution.py:75
  48.7 2.0 fusion.17
  50.7 7.7 %all-to-all-start = ((bf16[32,16,2048]{2,1,0:T(8,128)(2,1)}), bf16[32,16,2048]{2,1,0:T(8,128)(2,1)S(1)}, u32[]{:S(2)}, u32[]{:S(2)}) async-start(bf16[32,16,2048]{2,1,0:T(8,128)(2,1)} %fusion.17), calls=%async_computation | async-start | bytes 4194304 | tf_op jit(solution)/shard_map/all_to_all | solution.py:112
  58.5 0.1 copy.34
  58.6 0.1 broadcast_in_dim.51
  58.7 0.3 select_reduce_fusion.1
  59.0 28.7 %all_gather.10 = bf16[128,2048]{1,0:T(8,128)(2,1)S(1)} all-gather(bf16[128,128]{1,0:T(8,128)(2,1)S(1)} %copy-done.12), channel_id=1, replica_groups=mesh['dp'=32,'expert'=16] {'expert'}, dimensions={1}, use_global_device_ids=true | all-gather | bytes 557056 | tf_op jit(solution)/shard_map/all_gather | solution.py:76
  87.7 2.0 multiply_convert_fusion
  89.7 7.4 %all-to-all-start.1 = ((bf16[32,16,2048]{2,1,0:T(8,128)(2,1)}), bf16[32,16,2048]{2,1,0:T(8,128)(2,1)}, u32[]{:S(2)}, u32[]{:S(2)}) async-start(bf16[32,16,2048]{2,1,0:T(8,128)(2,1)} %bitcast.70), calls=%async_computation.1 | async-start | bytes 4194304 | tf_op jit(solution)/shard_map/all_to_all | solution.py:113
  97.2 0.0 reduce-scatter.2.cloned.1.call-start
  97.2 0.0 copy-start.7
  97.2 2.1 fusion.15
  99.3 0.0 copy-start.14
  99.3 1.6 multiply_convert_fusion.3
  100.9 0.7 copy-done.9
  101.6 2.1 convolution_convert_fusion
  103.7 19.5 %all-to-all-done.1 = bf16[32,16,2048]{2,1,0:T(8,128)(2,1)} async-done(((bf16[32,16,2048]{2,1,0:T(8,128)(2,1)}), bf16[32,16,2048]{2,1,0:T(8,128)(2,1)}, u32[]{:S(2)}, u32[]{:S(2)}) %all-to-all-start.1) | async-done | bytes 2097184 | tf_op jit(solution)/shard_map/all_to_all | solution.py:113
  123.2 2.7 %multiply_convert_fusion.1 = (bf16[512,192]{0,1:T(8,128)(2,1)S(1)}, bf16[512,192]{0,1:T(8,128)(2,1)S(1)}) fusion(f32[512,192]{0,1:T(8,128)} %copy-done.14, f32[512,192]{0,1:T(8,128)} %get-tuple-element.25, bf16[512,2048]{1,0:T(8,128)(2,1)} %bitcast.7, bf16[1,192,2048]{2,1,0:T(8,128)(2,1)S(1)} %copy-done), kind=kOutput, calls=%fused_computation.35 | convolution fusion | flops 403931136 | bytes 4063232 | tf_op jit(solution)/shard_map/dot_general | solution.py:17
  125.9 0.0 copy-start.11
  125.9 0.7 fusion.13
  126.7 0.5 copy-done.8
  127.2 0.8 add_convert_fusion
  128.0 0.8 copy-done.3
  128.8 0.6 pad_maximum_fusion
  129.4 54.6 %all_to_all.15 = bf16[32,32,2048]{2,1,0:T(8,128)(2,1)S(1)} all-to-all(bf16[32,32,2048]{2,1,0:T(8,128)(2,1)S(1)} %pad_maximum_fusion), channel_id=1, replica_groups=mesh['dp'=32,'expert'=16] {'dp'}, dimensions={0} | all-to-all | bytes 8388608 | tf_op jit(solution)/shard_map/all_to_all | solution.py:121
  183.9 0.6 fusion.39
  184.5 1.1 convolution_bitcast_fusion
  185.7 0.5 convolution_bitcast_fusion.1
  186.2 1.4 pad_maximum_fusion.1
  187.6 0.0 reduce-scatter.2.cloned.1.call-update
  187.7 2.4 fusion.2
  190.1 1.5 fusion.1
  191.6 3.2 %fusion.3 = bf16[1,192,2048]{2,1,0:T(8,128)(2,1)} fusion(bf16[512,192]{0,1:T(8,128)(2,1)S(1)} %copy-done.10, bf16[512,2048]{1,0:T(8,128)(2,1)} %bitcast.7), kind=kOutput, calls=%fused_computation.14 | convolution fusion | flops 403046400 | bytes 3080192 | tf_op jit(solution)/shard_map/dot_general | solution.py:23
  194.8 0.8 multiply_reduce_fusion
  195.6 0.3 select_reduce_fusion
  195.9 0.1 all_gather_reshape.3
  196.0 28.4 %all_gather.11 = f32[16,128,8]{1,2,0:T(8,128)S(1)} all-gather(f32[1,128,8]{1,2,0:T(8,128)S(1)} %copy.35), channel_id=1, replica_groups=mesh['dp'=32,'expert'=16] {'expert'}, dimensions={0}, use_global_device_ids=true | all-gather | bytes 69632 | tf_op jit(solution)/shard_map/all_gather | solution.py:153
  224.5 0.6 fusion.36
  225.1 31.6 %reduce-scatter.2.cloned.1.call-done = f32[2,128,128]{2,1,0:T(8,128)} async-done(((f32[2,128,2048]{2,1,0:T(8,128)}), f32[2,128,128]{2,1,0:T(8,128)}) %reduce-scatter.2.cloned.1.call-update) | async-done | bytes 131088 | tf_op jit(solution)/shard_map/reduce_scatter | solution.py:150
  256.7 0.9 convert.4
  257.6 0.6 slice_bitcast_fusion
  (30 shorter events, 0.2 us)
Async XLA Ops:
  7.2 94.4 %copy-start = (bf16[1,192,2048]{2,1,0:T(8,128)(2,1)S(1)}, bf16[1,192,2048]{2,1,0:T(8,128)(2,1)}, u32[]{:S(2)}) copy-start(bf16[1,192,2048]{2,1,0:T(8,128)(2,1)} %param.13) | copy-start | bytes 2359300
  50.7 7.8 %copy-start.13 = (f32[128,8]{0,1:T(8,128)S(1)}, f32[128,8]{0,1:T(8,128)}, u32[]{:S(2)}) copy-start(f32[128,8]{0,1:T(8,128)} %param.10) | copy-start | bytes 12292
  50.7 8.3 %copy-start.12 = (bf16[128,128]{1,0:T(8,128)(2,1)S(1)}, bf16[128,128]{1,0:T(8,128)(2,1)}, u32[]{:S(2)}) copy-start(bf16[128,128]{1,0:T(8,128)(2,1)} %param.8) | copy-start | bytes 98308
  50.7 39.0 %all-to-all-start = ((bf16[32,16,2048]{2,1,0:T(8,128)(2,1)}), bf16[32,16,2048]{2,1,0:T(8,128)(2,1)S(1)}, u32[]{:S(2)}, u32[]{:S(2)}) async-start(bf16[32,16,2048]{2,1,0:T(8,128)(2,1)} %fusion.17), calls=%async_computation | async-start | bytes 4194304 | tf_op jit(solution)/shard_map/all_to_all | solution.py:112
  89.7 33.4 %all-to-all-start.1 = ((bf16[32,16,2048]{2,1,0:T(8,128)(2,1)}), bf16[32,16,2048]{2,1,0:T(8,128)(2,1)}, u32[]{:S(2)}, u32[]{:S(2)}) async-start(bf16[32,16,2048]{2,1,0:T(8,128)(2,1)} %bitcast.70), calls=%async_computation.1 | async-start | bytes 4194304 | tf_op jit(solution)/shard_map/all_to_all | solution.py:113
  97.2 159.5 %reduce-scatter.2.cloned.1.call-start = ((), (), s32[]{:S(2)}) async-start(), calls=%async_computation.4 | async-start | bytes 2228224 | tf_op jit(solution)/shard_map/reduce_scatter | solution.py:150
  97.2 2.1 copy-start.7
  99.3 1.6 copy-start.14
  100.9 0.7 copy-start.9
  123.2 2.8 %copy-start.6 = (bf16[1,192,2048]{2,1,0:T(8,128)(2,1)S(1)}, bf16[1,192,2048]{2,1,0:T(8,128)(2,1)}, u32[]{:S(2)}) copy-start(bf16[1,192,2048]{2,1,0:T(8,128)(2,1)} %param.11) | copy-start | bytes 2359300
  125.9 0.8 copy-start.4
  125.9 0.8 copy-start.11
  125.9 1.3 copy-start.8
  127.2 1.6 copy-start.3
  184.5 1.7 copy-start.1
  187.7 2.4 copy-start.5
  190.1 1.5 copy-start.10
  191.6 3.2 %copy-start.2 = (bf16[32,16,2048]{2,1,0:T(8,128)(2,1)S(1)}, bf16[32,16,2048]{2,1,0:T(8,128)(2,1)}, u32[]{:S(2)}) copy-start(bf16[32,16,2048]{2,1,0:T(8,128)(2,1)} %copy-done.1) | copy-start | bytes 6291460
Sparse Core Ops, SparseCore 0:
  187.8 68.8 reduce-scatter.1
where the time goes:
time: 266 us; the launch traced here: 265 us
  blocking collectives  151 us (57%)
  waiting for transfers between devices  51.1 us (19%)
  matrix products  24 us (9%)
  starting transfers between devices  15.2 us (6%)
  between operations  14.3 us (5%)
  other arithmetic  5.18 us (2%)
  local copies, waits for them, and re-layouts  4.67 us (2%)
    all_to_all x1, blocking collectives, per_device(): lax.all_to_all(jnp.concatenate([part_out.reshape(dp_count, capacity, feat...  54.6 us
    all_gather x1, blocking collectives, per_device(): full_x = lax.all_gather(tokens, 'expert', axis=1, tiled=True)  38.8 us
    reduce_scatter x1, waiting for transfers between devices, per_device(): lax.psum_scatter(jnp.stack([out_part, grad_part]), 'expert', scatter_dime...  31.6 us
    all_gather x1, blocking collectives, per_device(): full_dy = lax.all_gather(cotangent, 'expert', axis=1, tiled=True)  28.7 us
    all_gather x1, blocking collectives, per_device(): gate_all = lax.all_gather(gate_part, 'expert', axis=0, tiled=False)  28.4 us
    all_to_all x1, waiting for transfers between devices, per_device(): lax.all_to_all(send_do, 'dp', split_axis=0, concat_axis=0, tiled=True)  19.5 us
    all_to_all x1, starting transfers between devices, per_device(): lax.all_to_all(send_x, 'dp', split_axis=0, concat_axis=0, tiled=True)  7.74 us
    dot_general x4, matrix products, contract_first(): lax.dot_general(first_op, second_op, (((0,), (0,)), ((), ())), preferred_...  7.59 us
  transfers between devices with their start and end apart: 3, of which 2 were waited for; matrix products, arithmetic and copies ran while one was open for 6% of the time, Pallas kernels for 0%

commit v1 on v0

--- a/solution.py
+++ b/solution.py
@@ -72,8 +72,11 @@
 
 
 def per_device(tokens, cotangent, expert_ids, gate_weights, w_gate, w_up, w_down):
-    full_x = lax.all_gather(tokens, "expert", axis=1, tiled=True)
-    full_dy = lax.all_gather(cotangent, "expert", axis=1, tiled=True)
+    full_x, full_dy = jnp.split(
+        lax.all_gather(jnp.concatenate([tokens, cotangent], axis=0), "expert", axis=1, tiled=True),
+        [tokens.shape[0]],
+        axis=0,
+    )
     dp_count = lax.axis_size("dp")
     column_count = lax.axis_size("expert")
     column = lax.axis_index("expert")

time: 266 us -> 299 us (1.12)
  the two profiles are of different devices: /device:TPU:4 before, /device:TPU:10 now
where the time goes in v1:
time: 299 us; the launch traced here: 298 us
  waiting for transfers between devices  150 us (50%)
  blocking collectives  82.6 us (28%)
  matrix products  25.2 us (8%)
  starting transfers between devices  15.5 us (5%)
  between operations  14.3 us (5%)
  other arithmetic  6.66 us (2%)
  local copies, waits for them, and re-layouts  3.8 us (1%)
    all_gather x1, waiting for transfers between devices, per_device(): lax.all_gather(jnp.concatenate([tokens, cotangent], axis=0), 'expert', ax...  75.9 us
    all_to_all x1, blocking collectives, per_device(): lax.all_to_all(jnp.concatenate([part_out.reshape(dp_count, capacity, feat...  54.4 us
    reduce_scatter x1, waiting for transfers between devices, per_device(): lax.psum_scatter(jnp.stack([out_part, grad_part]), 'expert', scatter_dime...  32.3 us
    all_gather x1, blocking collectives, per_device(): gate_all = lax.all_gather(gate_part, 'expert', axis=0, tiled=False)  28.2 us
    all_to_all x1, waiting for transfers between devices, per_device(): lax.all_to_all(send_x, 'dp', split_axis=0, concat_axis=0, tiled=True)  22.1 us
    all_to_all x1, waiting for transfers between devices, per_device(): lax.all_to_all(send_do, 'dp', split_axis=0, concat_axis=0, tiled=True)  20 us
    all_to_all x1, starting transfers between devices, per_device(): lax.all_to_all(send_do, 'dp', split_axis=0, concat_axis=0, tiled=True)  7.85 us
    all_to_all x1, starting transfers between devices, per_device(): lax.all_to_all(send_x, 'dp', split_axis=0, concat_axis=0, tiled=True)  7.53 us
  transfers between devices with their start and end apart: 4, of which 4 were waited for; matrix products, arithmetic and copies ran while one was open for 7% of the time, Pallas kernels for 0%

profile of v1, /device:TPU:10, one launch (start us, length us, event | category | flops | bytes accessed | tf_op | source)
XLA Modules:
  0.0 298.4 jit_solution(12886813966229635066)
XLA Ops:
  7.2 0.0 copy-start
  7.2 0.0 all-gather.2.cloned.1.call-start
  7.2 1.5 pad_maximum_fusion.2
  8.7 0.0 all-gather.2.cloned.1.call-update
  8.7 0.8 copy.28
  9.5 0.1 reshape.163
  9.7 0.5 fusion.6
  10.2 0.1 convert_element_type.69
  10.3 0.1 fusion.31
  10.4 0.9 fusion.4
  11.3 75.9 %all-gather.2.cloned.1.call-done = bf16[256,2048]{1,0:T(8,128)(2,1)} async-done(((bf16[256,128]{1,0:T(8,128)(2,1)}), bf16[256,2048]{1,0:T(8,128)(2,1)}) %all-gather.2.cloned.1.call-update) | async-done | bytes 1048592 | tf_op jit(solution)/shard_map/all_gather | solution.py:76
  87.3 3.1 %fusion.17 = bf16[32,16,2048]{2,1,0:T(8,128)(2,1)} fusion(pred[32,16,128]{2,1,0:T(8,128)(4,1)S(1)} %bitcast.74, bf16[256,2048]{1,0:T(8,128)(2,1)} %all-gather.2.cloned.1.call-done), kind=kOutput, calls=%fused_computation.34 | convolution fusion | flops 268435456 | bytes 2686976 | tf_op jit(solution)/shard_map/dot_general | solution.py:107
  90.4 7.5 %all-to-all-start = ((bf16[32,16,2048]{2,1,0:T(8,128)(2,1)}), bf16[32,16,2048]{2,1,0:T(8,128)(2,1)S(1)}, u32[]{:S(2)}, u32[]{:S(2)}) async-start(bf16[32,16,2048]{2,1,0:T(8,128)(2,1)} %fusion.17), calls=%async_computation | async-start | bytes 4194304 | tf_op jit(solution)/shard_map/all_to_all | solution.py:115
  97.9 0.1 copy.34
  98.0 0.1 broadcast_in_dim.51
  98.1 0.3 select_reduce_fusion.1
  98.4 3.1 %multiply_convert_fusion = bf16[512,2048]{1,0:T(8,128)(2,1)} fusion(pred[512,128]{1,0:T(8,128)(4,1)S(1)} %fusion.4, f32[512]{0:T(512)S(1)} %select_reduce_fusion.1, bf16[256,2048]{1,0:T(8,128)(2,1)} %all-gather.2.cloned.1.call-done), kind=kOutput, calls=%fused_computation.3 | convolution fusion | flops 270532608 | bytes 2689024 | tf_op jit(solution)/shard_map/dot_general | solution.py:110
  101.5 22.1 %all-to-all-done = bf16[32,16,2048]{2,1,0:T(8,128)(2,1)S(1)} async-done(((bf16[32,16,2048]{2,1,0:T(8,128)(2,1)}), bf16[32,16,2048]{2,1,0:T(8,128)(2,1)S(1)}, u32[]{:S(2)}, u32[]{:S(2)}) %all-to-all-start) | async-done | bytes 2097184 | tf_op jit(solution)/shard_map/all_to_all | solution.py:115
  123.6 7.9 %all-to-all-start.1 = ((bf16[32,16,2048]{2,1,0:T(8,128)(2,1)}), bf16[32,16,2048]{2,1,0:T(8,128)(2,1)}, u32[]{:S(2)}, u32[]{:S(2)}) async-start(bf16[32,16,2048]{2,1,0:T(8,128)(2,1)} %bitcast.68), calls=%async_computation.1 | async-start | bytes 4194304 | tf_op jit(solution)/shard_map/all_to_all | solution.py:116
  131.5 0.0 reduce-scatter.2.cloned.1.call-start
  131.5 0.0 copy-start.6
  131.5 2.1 fusion.15
  133.6 1.6 multiply_convert_fusion.3
  135.2 2.1 convolution_convert_fusion
  137.3 20.0 %all-to-all-done.1 = bf16[32,16,2048]{2,1,0:T(8,128)(2,1)} async-done(((bf16[32,16,2048]{2,1,0:T(8,128)(2,1)}), bf16[32,16,2048]{2,1,0:T(8,128)(2,1)}, u32[]{:S(2)}, u32[]{:S(2)}) %all-to-all-start.1) | async-done | bytes 2097184 | tf_op jit(solution)/shard_map/all_to_all | solution.py:116
  157.3 2.7 multiply_convert_fusion.1
  160.1 0.7 fusion.13
  160.8 0.4 copy-done.7
  161.2 0.8 add_convert_fusion
  161.9 0.8 copy-done.3
  162.8 0.6 pad_maximum_fusion
  163.3 54.4 %all_to_all.15 = bf16[32,32,2048]{2,1,0:T(8,128)(2,1)S(1)} all-to-all(bf16[32,32,2048]{2,1,0:T(8,128)(2,1)S(1)} %pad_maximum_fusion), channel_id=1, replica_groups=mesh['dp'=32,'expert'=16] {'dp'}, dimensions={0} | all-to-all | bytes 8388608 | tf_op jit(solution)/shard_map/all_to_all | solution.py:124
  217.7 0.6 fusion.40
  218.3 1.1 convolution_bitcast_fusion
  219.5 0.5 convolution_bitcast_fusion.1
  220.0 1.5 pad_maximum_fusion.1
  221.4 0.0 reduce-scatter.2.cloned.1.call-update
  221.5 1.5 fusion.2
  222.9 1.5 fusion.1
  224.4 3.2 %fusion.3 = bf16[1,192,2048]{2,1,0:T(8,128)(2,1)} fusion(bf16[512,192]{0,1:T(8,128)(2,1)S(1)} %get-tuple-element.11, bf16[512,2048]{1,0:T(8,128)(2,1)} %bitcast.7), kind=kOutput, calls=%fused_computation.14 | convolution fusion | flops 403046400 | bytes 3080192 | tf_op jit(solution)/shard_map/dot_general | solution.py:23
  227.6 0.8 multiply_reduce_fusion
  228.4 0.3 select_reduce_fusion
  228.7 0.1 all_gather_reshape.3
  228.9 28.2 %all_gather.7 = f32[16,128,8]{1,2,0:T(8,128)S(1)} all-gather(f32[1,128,8]{1,2,0:T(8,128)S(1)} %copy.35), channel_id=1, replica_groups=mesh['dp'=32,'expert'=16] {'expert'}, dimensions={0}, use_global_device_ids=true | all-gather | bytes 69632 | tf_op jit(solution)/shard_map/all_gather | solution.py:156
  257.1 0.6 fusion.37
  257.7 32.3 %reduce-scatter.2.cloned.1.call-done = f32[2,128,128]{2,1,0:T(8,128)} async-done(((f32[2,128,2048]{2,1,0:T(8,128)}), f32[2,128,128]{2,1,0:T(8,128)}) %reduce-scatter.2.cloned.1.call-update) | async-done | bytes 131088 | tf_op jit(solution)/shard_map/reduce_scatter | solution.py:153
  290.0 0.9 convert.4
  290.9 0.6 slice_bitcast_fusion.2
  (22 shorter events, 0.2 us)
Async XLA Ops:
  7.2 128.1 %copy-start = (bf16[1,192,2048]{2,1,0:T(8,128)(2,1)S(1)}, bf16[1,192,2048]{2,1,0:T(8,128)(2,1)}, u32[]{:S(2)}) copy-start(bf16[1,192,2048]{2,1,0:T(8,128)(2,1)} %param.13) | copy-start | bytes 2359300
  7.2 80.1 %all-gather.2.cloned.1.call-start = ((), (), s32[]{:S(2)}) async-start(), calls=%async_computation.4 | async-start | bytes 1114112 | tf_op jit(solution)/shard_map/all_gather | solution.py:76
  90.3 7.5 %copy-start.8 = (f32[128,8]{0,1:T(8,128)S(1)}, f32[128,8]{0,1:T(8,128)}, u32[]{:S(2)}) copy-start(f32[128,8]{0,1:T(8,128)} %param.10) | copy-start | bytes 12292
  90.4 33.3 %all-to-all-start = ((bf16[32,16,2048]{2,1,0:T(8,128)(2,1)}), bf16[32,16,2048]{2,1,0:T(8,128)(2,1)S(1)}, u32[]{:S(2)}, u32[]{:S(2)}) async-start(bf16[32,16,2048]{2,1,0:T(8,128)(2,1)} %fusion.17), calls=%async_computation | async-start | bytes 4194304 | tf_op jit(solution)/shard_map/all_to_all | solution.py:115
  123.6 33.7 %all-to-all-start.1 = ((bf16[32,16,2048]{2,1,0:T(8,128)(2,1)}), bf16[32,16,2048]{2,1,0:T(8,128)(2,1)}, u32[]{:S(2)}, u32[]{:S(2)}) async-start(bf16[32,16,2048]{2,1,0:T(8,128)(2,1)} %bitcast.68), calls=%async_computation.1 | async-start | bytes 4194304 | tf_op jit(solution)/shard_map/all_to_all | solution.py:116
  131.5 158.5 %reduce-scatter.2.cloned.1.call-start = ((), (), s32[]{:S(2)}) async-start(), calls=%async_computation.5 | async-start | bytes 2228224 | tf_op jit(solution)/shard_map/reduce_scatter | solution.py:153
  131.5 2.1 copy-start.6
  133.6 1.6 copy-start.9
  157.3 2.7 copy-start.5
  160.0 1.1 copy-start.7
  161.2 1.6 copy-start.3
  218.3 1.7 copy-start.1
  222.9 4.7 %copy-start.4 = (bf16[256,2048]{1,0:T(8,128)(2,1)S(1)}, bf16[256,2048]{1,0:T(8,128)(2,1)}, u32[]{:S(2)}) copy-start(bf16[256,2048]{1,0:T(8,128)(2,1)} %all-gather.2.cloned.1.call-done) | copy-start | bytes 3145732
  224.4 3.2 %copy-start.2 = (bf16[32,16,2048]{2,1,0:T(8,128)(2,1)S(1)}, bf16[32,16,2048]{2,1,0:T(8,128)(2,1)}, u32[]{:S(2)}) copy-start(bf16[32,16,2048]{2,1,0:T(8,128)(2,1)} %copy-done.1) | copy-start | bytes 6291460
Sparse Core Ops, SparseCore 0:
  10.6 76.6 all-gather.1
  221.6 68.3 reduce-scatter.1
